TPU v7x, 256 devices: a whole 4x4x8 slice. The times are simulated.
256 devices in a mesh: rows: 16 (over y, x), cols: 8 (over z), depth: 2 (over core).
Axes of the slice: x: 4, y: 4, z: 8, core: 2. Of those that a mesh axis runs over, the one named last changes fastest.
Arguments:
- tile_left: float32 [16, 8, 64, 2048], P('rows', 'cols'), may hold values from -6 to 6
- tile_right: float32 [16, 8, 64, 2048], P('rows', 'cols'), may hold values from -0.75 to 0.75
- left_u: bfloat16 [2, 16, 16, 64, 2048], P('depth', 'cols', 'rows'), may hold values from -6 to 6
- left_v: bfloat16 [2, 16, 16, 64, 2048], P('depth', 'cols', 'rows'), may hold values from -0.0625 to 0.0625
- rank_left: int32 [2, 16, 16], P('depth', 'cols', 'rows'), may hold values from 16 to 64
- right_u: bfloat16 [2, 16, 8, 64, 2048], P('depth', 'rows', 'cols'), may hold values from -6 to 6
- right_v: bfloat16 [2, 16, 8, 64, 2048], P('depth', 'rows', 'cols'), may hold values from -0.0625 to 0.0625
- rank_right: int32 [2, 16, 8], P('depth', 'rows', 'cols'), may hold values from 16 to 64
- triples: int32 [16, 8, 2, 6], P('rows', 'cols', 'depth'), may hold values from -1 to 15, as said below
Outputs:
- new_left: float32 [16, 8, 64, 2048], P('rows', 'cols', None, 'depth')
- new_right: float32 [16, 8, 64, 2048], P('rows', 'cols', None, 'depth')
Inputs may be any that keep to these rules, and one draw needn't show every extreme that they name: `triples`: for each tile and layer the first entries are distinct panel numbers of 0 to 15 and the remaining entries are -1; every list has at least one panel number, and in every draw some tile in some layer lists all 6.
All inputs are finite; a program needn't handle non-finite values.
Results may differ from a plain program's by a relative error of at most 0.0043.
Values may be sent and summed in bfloat16 or wider, within the bound.
No kernel may reach another device: no remote copies, remote signals or barrier semaphores. Data moves between devices by JAX's collectives and lax.ppermute only.
A program may use at most 128 MiB of HBM per device.

v0:
```python
import math
import jax
import jax.numpy as jnp
from jax import lax
from jax.sharding import PartitionSpec as P

NB = 2048
RK = 64
HIGHEST = lax.Precision.HIGHEST


def swapped(block, axis, apart):
    count = lax.axis_size(axis)
    route = []
    for low in range(count):
        high = low | 1 << apart
        if high != low and high < count:
            route += [(low, high), (high, low)]
    return lax.ppermute(block, axis, route)


def cross(first, second, dim_first, dim_second):
    return lax.dot_general(
        first,
        second,
        (((dim_first,), (dim_second,)), ((), ())),
        precision=HIGHEST,
        preferred_element_type=jnp.float32,
    )


def start_rows(rank, width):
    freq = lax.broadcasted_iota(jnp.int32, (rank, width), 0) + 1
    cell = 2 * lax.broadcasted_iota(jnp.int32, (rank, width), 1) + 1
    phase = freq * cell % (4 * width)
    return jnp.cos(phase.astype(jnp.float32) * (math.pi / (2 * width)))


def orthonormal(rows_t):
    gram = cross(rows_t, rows_t, 1, 1)
    shift = 1e-05 * jnp.trace(gram) / gram.shape[0] + 1e-06
    gram = gram + shift * jnp.eye(gram.shape[0], dtype=gram.dtype)
    lower = lax.linalg.cholesky(gram)
    return lax.linalg.triangular_solve(lower, rows_t, left_side=True, lower=True)


def compress(left_t, right_t):
    probe = start_rows(RK, NB)
    for sweep in range(2):
        first = cross(left_t, probe, 1, 1)
        image = orthonormal(cross(first, right_t, 0, 0))
        second = cross(right_t, image, 1, 1)
        probe = orthonormal(cross(second, left_t, 0, 0))
    first = cross(left_t, probe, 1, 1)
    return (probe, cross(first, right_t, 0, 0))


def slot_term(outer_left, inner_left, rank_l, inner_right, rank_r):
    inner = lax.dot_general(
        inner_left, inner_right, (((1,), (1,)), ((), ())), preferred_element_type=jnp.float32
    )
    index = jnp.arange(RK)
    keep = (index[:, None] < rank_l) & (index[None, :] < rank_r)
    inner = jnp.where(keep, inner, 0.0).astype(jnp.bfloat16)
    return -lax.dot_general(
        inner, outer_left, (((0,), (0,)), ((), ())), preferred_element_type=jnp.float32
    )


def shards(tile_left, tile_right, left_u, left_v, rank_left, right_u, right_v, rank_right, triples):
    layers = lax.axis_size("depth")
    tcols = tile_left.shape[1]
    slots = triples.shape[3]
    row_u, row_v, row_rank = (
        lax.all_gather(left_u, "cols", axis=1, tiled=True),
        lax.all_gather(left_v, "cols", axis=1, tiled=True),
        lax.all_gather(rank_left, "cols", axis=1, tiled=True),
    )
    col_u, col_v, col_rank = (
        lax.all_gather(right_u, "rows", axis=1, tiled=True),
        lax.all_gather(right_v, "rows", axis=1, tiled=True),
        lax.all_gather(rank_right, "rows", axis=1, tiled=True),
    )
    term_list = []
    base_list = []
    tile = 0
    for slot in range(slots):
        panel = triples[0, tile, 0, slot]
        valid = panel >= 0
        chosen = jnp.maximum(panel, 0)
        term_list.append(
            lax.cond(
                valid,
                lambda: slot_term(
                    row_u[0, chosen, 0],
                    row_v[0, chosen, 0],
                    row_rank[0, chosen, 0],
                    col_v[0, chosen, tile],
                    col_rank[0, chosen, tile],
                ),
                lambda: jnp.zeros((RK, NB), jnp.float32),
            )
        )
        base_list.append(
            jnp.where(valid, col_u[0, chosen, tile], jnp.zeros((RK, NB), jnp.bfloat16))
        )
    terms = jnp.stack(term_list).reshape(tcols, slots, RK, NB)
    bases = jnp.stack(base_list).reshape(tcols, slots, RK, NB)
    probes = []
    images = []
    tile = 0
    left_t = jnp.concatenate(
        [tile_left[0, tile] / layers, terms[tile].reshape(slots * RK, NB)], axis=0
    )
    right_t = jnp.concatenate(
        [tile_right[0, tile], bases[tile].astype(jnp.float32).reshape(slots * RK, NB)], axis=0
    )
    probe, image = compress(left_t, right_t)
    probes.append(probe)
    images.append(image)
    probes = jnp.stack(probes)
    images = jnp.stack(images)
    layer_index = lax.axis_index("depth")
    other_probes, other_images = swapped((probes, images), "depth", 0)
    lower_side = layer_index >> 0 & 1 == 0
    first_probes = jnp.where(lower_side, probes, other_probes)
    second_probes = jnp.where(lower_side, other_probes, probes)
    first_images = jnp.where(lower_side, images, other_images)
    second_images = jnp.where(lower_side, other_images, images)
    tile = 0
    probe, image = compress(
        jnp.concatenate([first_probes[tile], second_probes[tile]], axis=0),
        jnp.concatenate([first_images[tile], second_images[tile]], axis=0),
    )
    joined_probes = [probe]
    joined_images = [image]
    probes = jnp.stack(joined_probes)
    images = jnp.stack(joined_images)
    share = NB // layers
    offset = layer_index * share
    new_left = lax.dynamic_slice_in_dim(probes * math.sqrt(NB), offset, share, 2).reshape(
        1, tcols, RK, share
    )
    new_right = lax.dynamic_slice_in_dim(images / math.sqrt(NB), offset, share, 2).reshape(
        1, tcols, RK, share
    )
    return (new_left, new_right)


def solution(mesh):
    in_specs = (
        P("rows", "cols", None, None),
        P("rows", "cols", None, None),
        P("depth", "cols", "rows", None, None),
        P("depth", "cols", "rows", None, None),
        P("depth", "cols", "rows"),
        P("depth", "rows", "cols", None, None),
        P("depth", "rows", "cols", None, None),
        P("depth", "rows", "cols"),
        P("rows", "cols", "depth", None),
    )
    out_specs = (P("rows", "cols", None, "depth"), P("rows", "cols", None, "depth"))
    return jax.shard_map(shards, mesh=mesh, in_specs=in_specs, out_specs=out_specs, check_vma=False)
```

profile of v0, /device:TPU:57, one launch (start us, length us, event | category | flops | bytes accessed | tf_op | source)
XLA Modules:
  0.0 460.7 jit_solution(14910221890863665000)
XLA Ops:
  12.6 10.3 %all-reduce.1 = s32[16]{0:T(128)S(1)} all-reduce(s32[16]{0:T(128)S(1)} %bitcast_dynamic-update-slice_fusion.6), channel_id=1, replica_groups=mesh['rows'=16,'cols'=8,'depth'=2] {'rows'}, use_global_device_ids=true, to_apply=%add.1 | all-reduce | flops 16 | bytes 128
  34.9 13.5 %all-reduce = s32[16]{0:T(128)S(1)} all-reduce(s32[16]{0:T(128)S(1)} %bitcast_dynamic-update-slice_fusion.7), channel_id=1, replica_groups=mesh['rows'=16,'cols'=8,'depth'=2] {'cols'}, use_global_device_ids=true, to_apply=%add | all-reduce | flops 16 | bytes 128
  50.2 15.1 %all-gather.5.cloned.1.call-done = bf16[1,16,1,64,2048]{4,3,2,0,1:T(8,128)(2,1)} async-done(((bf16[1,2,1,64,2048]{4,3,2,0,1:T(8,128)(2,1)}), bf16[1,16,1,64,2048]{4,3,2,0,1:T(8,128)(2,1)}) %all-gather.5.cloned.1.call-update) | async-done | bytes 4194320 | tf_op jit(solution)/shard_map/all_gather | solution.py:76
  65.3 55.2 %all-gather.9.cloned.1.call-done = bf16[1,16,1,64,2048]{4,3,2,0,1:T(8,128)(2,1)} async-done(((bf16[1,2,1,64,2048]{4,3,2,0,1:T(8,128)(2,1)}), bf16[1,16,1,64,2048]{4,3,2,0,1:T(8,128)(2,1)}) %all-gather.9.cloned.1.call-update) | async-done | bytes 4194320 | tf_op jit(solution)/shard_map/all_gather | solution.py:75
  120.4 59.2 %all-gather.7.cloned.1.call-done = bf16[1,16,1,64,2048]{4,3,2,0,1:T(8,128)(2,1)} async-done(((bf16[1,1,1,64,2048]{4,3,2,0,1:T(8,128)(2,1)}), bf16[1,16,1,64,2048]{4,3,2,0,1:T(8,128)(2,1)}) %all-gather.7.cloned.1.call-update) | async-done | bytes 4194320 | tf_op jit(solution)/shard_map/all_gather | solution.py:81
  179.7 3.5 conditional.6
  184.0 54.2 %all-gather.11.cloned.1.call-done = bf16[1,16,1,64,2048]{4,3,2,0,1:T(8,128)(2,1)} async-done(((bf16[1,1,1,64,2048]{4,3,2,0,1:T(8,128)(2,1)}), bf16[1,16,1,64,2048]{4,3,2,0,1:T(8,128)(2,1)}) %all-gather.11.cloned.1.call-update) | async-done | bytes 4194320 | tf_op jit(solution)/shard_map/all_gather | solution.py:80
  244.7 4.4 conditional.7
  246.6 2.5 fusion.19
  251.0 4.4 conditional.8
  252.9 2.5 fusion.38
  255.4 1.9 constant_dynamic-update-slice_fusion.3
  257.3 4.4 conditional.9
  259.2 2.5 fusion.57
  261.7 1.9 constant_dynamic-update-slice_fusion.2
  263.6 4.4 conditional.10
  265.5 2.5 fusion.76
  269.9 4.8 %conditional.11 = (f32[1,64,2048]{2,1,0:T(8,128)}) conditional(s32[]{:T(128)} %convert_element_type.62, () %tuple.68, (s32[]{:T(128)}, s32[1,16,1]{1,2,0:T(1,128)S(1)}, s32[1,16,1]{1,2,0:T(1,128)S(1)}, bf16[1,16,1,64,2048]{4,3,2,0,1:T(8,128)(2,1)}, bf16[1,16,1,64,2048]{4,3,2,0,1:T(8,128)(2,1)}, ...), branch_computations={%region_10.11_spmd, %region_11.12_spmd} | conditional | flops 33697924 | bytes 1312582 | solution.py:92
  271.8 2.5 fusion.95
  274.7 2.0 constant_dynamic-update-slice_fusion
  276.7 6.9 %fusion.122 = f32[448,64]{1,0:T(8,128)S(1)} fusion(f32[384,2048]{1,0:T(8,128)} %bitcast.304, f32[64,2048]{1,0:T(8,128)} %multiply_bitcast_fusion, s32[2048]{0:T(1024)S(1)} %multiply_add_fusion, s32[64]{0:T(128)S(1)} %iota_add_fusion), kind=kOutput, calls=%fused_computation.132 | convolution fusion | flops 707395584 | bytes 3793152 | tf_op jit(solution)/shard_map/dot_general | solution.py:23
  283.6 2.4 fusion.117
  288.7 5.8 %custom-call.20 = f32[64,64]{1,0:T(8,128)S(1)} custom-call(f32[64,64]{1,0:T(8,128)S(1)} %fusion.180), custom_call_target="Cholesky" | custom-call | tf_op jit(solution)/shard_map/cholesky/custom-call.1 | solution.py:43
  295.9 4.9 %custom-call.21 = f32[1,64,64]{1,2,0:T(8,128)S(1)} custom-call(f32[1,64,64]{2,1,0:T(8,128)S(1)} %fusion.141), custom_call_target="InvertDiagBlocksLowerTriangular" | custom-call | tf_op jit(solution)/shard_map/triangular_solve/custom-call.0 | solution.py:44
  302.6 4.2 fusion.116
  306.9 2.4 fusion.121
  312.0 5.8 %custom-call.22 = f32[64,64]{1,0:T(8,128)S(1)} custom-call(f32[64,64]{1,0:T(8,128)S(1)} %fusion.176), custom_call_target="Cholesky" | custom-call | tf_op jit(solution)/shard_map/cholesky/custom-call.1 | solution.py:43
  319.2 4.9 %custom-call.23 = f32[1,64,64]{1,2,0:T(8,128)S(1)} custom-call(f32[1,64,64]{2,1,0:T(8,128)S(1)} %fusion.142), custom_call_target="InvertDiagBlocksLowerTriangular" | custom-call | tf_op jit(solution)/shard_map/triangular_solve/custom-call.0 | solution.py:44
  325.9 5.0 %fusion.120 = f32[448,64]{1,0:T(8,128)S(1)} fusion(f32[64,2048]{1,0:T(8,128)S(1)} %fusion.173, f32[384,2048]{1,0:T(8,128)} %bitcast.305, f32[64,2048]{1,0:T(8,128)} %multiply_bitcast_fusion), kind=kOutput, calls=%fused_computation.130 | convolution fusion | flops 705560576 | bytes 4308992 | tf_op jit(solution)/shard_map/dot_general | solution.py:23
  330.9 2.4 fusion.115
  336.0 6.2 %custom-call.24 = f32[64,64]{1,0:T(8,128)S(1)} custom-call(f32[64,64]{1,0:T(8,128)S(1)} %fusion.172), custom_call_target="Cholesky" | custom-call | tf_op jit(solution)/shard_map/cholesky/custom-call.1 | solution.py:43
  343.6 4.9 %custom-call.25 = f32[1,64,64]{1,2,0:T(8,128)S(1)} custom-call(f32[1,64,64]{2,1,0:T(8,128)S(1)} %fusion.143), custom_call_target="InvertDiagBlocksLowerTriangular" | custom-call | tf_op jit(solution)/shard_map/triangular_solve/custom-call.0 | solution.py:44
  350.3 4.0 fusion.114
  354.4 2.4 fusion.119
  359.5 5.8 %custom-call.26 = f32[64,64]{1,0:T(8,128)S(1)} custom-call(f32[64,64]{1,0:T(8,128)S(1)} %fusion.168), custom_call_target="Cholesky" | custom-call | tf_op jit(solution)/shard_map/cholesky/custom-call.1 | solution.py:43
  366.7 4.9 %custom-call.27 = f32[1,64,64]{1,2,0:T(8,128)S(1)} custom-call(f32[1,64,64]{2,1,0:T(8,128)S(1)} %fusion.144), custom_call_target="InvertDiagBlocksLowerTriangular" | custom-call | tf_op jit(solution)/shard_map/triangular_solve/custom-call.0 | solution.py:44
  371.6 2.5 fusion.165
  374.1 5.2 %fusion.118 = f32[448,64]{1,0:T(8,128)S(1)} fusion(f32[64,2048]{1,0:T(8,128)} %fusion.165, f32[384,2048]{1,0:T(8,128)} %bitcast.306, f32[64,2048]{1,0:T(8,128)} %multiply_bitcast_fusion), kind=kOutput, calls=%fused_computation.128 | convolution fusion | flops 705560576 | bytes 4308992 | tf_op jit(solution)/shard_map/dot_general | solution.py:23
  379.3 2.4 convolution_bitcast_fusion
  383.8 3.0 fusion.131
  389.5 5.8 %custom-call.28 = f32[64,64]{1,0:T(8,128)S(1)} custom-call(f32[64,64]{1,0:T(8,128)S(1)} %fusion.164), custom_call_target="Cholesky" | custom-call | tf_op jit(solution)/shard_map/cholesky/custom-call.1 | solution.py:43
  396.7 4.9 %custom-call.29 = f32[1,64,64]{1,2,0:T(8,128)S(1)} custom-call(f32[1,64,64]{2,1,0:T(8,128)S(1)} %fusion.145), custom_call_target="InvertDiagBlocksLowerTriangular" | custom-call | tf_op jit(solution)/shard_map/triangular_solve/custom-call.0 | solution.py:44
  405.8 5.8 %custom-call.30 = f32[64,64]{1,0:T(8,128)S(1)} custom-call(f32[64,64]{1,0:T(8,128)S(1)} %fusion.160), custom_call_target="Cholesky" | custom-call | tf_op jit(solution)/shard_map/cholesky/custom-call.1 | solution.py:43
  413.0 4.9 %custom-call.31 = f32[1,64,64]{1,2,0:T(8,128)S(1)} custom-call(f32[1,64,64]{2,1,0:T(8,128)S(1)} %fusion.146), custom_call_target="InvertDiagBlocksLowerTriangular" | custom-call | tf_op jit(solution)/shard_map/triangular_solve/custom-call.0 | solution.py:44
  422.3 5.8 %custom-call.32 = f32[64,64]{1,0:T(8,128)S(1)} custom-call(f32[64,64]{1,0:T(8,128)S(1)} %fusion.156), custom_call_target="Cholesky" | custom-call | tf_op jit(solution)/shard_map/cholesky/custom-call.1 | solution.py:43
  429.5 4.9 %custom-call.33 = f32[1,64,64]{1,2,0:T(8,128)S(1)} custom-call(f32[1,64,64]{2,1,0:T(8,128)S(1)} %fusion.147), custom_call_target="InvertDiagBlocksLowerTriangular" | custom-call | tf_op jit(solution)/shard_map/triangular_solve/custom-call.0 | solution.py:44
  438.7 5.8 %custom-call.34 = f32[64,64]{1,0:T(8,128)S(1)} custom-call(f32[64,64]{1,0:T(8,128)S(1)} %fusion.152), custom_call_target="Cholesky" | custom-call | tf_op jit(solution)/shard_map/cholesky/custom-call.1 | solution.py:43
  445.9 4.9 %custom-call.35 = f32[1,64,64]{1,2,0:T(8,128)S(1)} custom-call(f32[1,64,64]{2,1,0:T(8,128)S(1)} %fusion.148), custom_call_target="InvertDiagBlocksLowerTriangular" | custom-call | tf_op jit(solution)/shard_map/triangular_solve/custom-call.0 | solution.py:44
  (140 shorter events, 76.3 us)
Async XLA Ops:
  7.2 58.1 %all-gather.5.cloned.1.call-start = ((), (), s32[]{:S(2)}) async-start(), calls=%async_computation | async-start | bytes 4718592 | tf_op jit(solution)/shard_map/all_gather | solution.py:76
  7.9 112.5 %all-gather.9.cloned.1.call-start = ((), (), s32[]{:S(2)}) async-start(), calls=%async_computation.2 | async-start | bytes 4718592 | tf_op jit(solution)/shard_map/all_gather | solution.py:75
  8.6 171.0 %all-gather.7.cloned.1.call-start = ((), (), s32[]{:S(2)}) async-start(), calls=%async_computation.1 | async-start | bytes 4456448 | tf_op jit(solution)/shard_map/all_gather | solution.py:81
  9.4 228.8 %all-gather.11.cloned.1.call-start = ((), (), s32[]{:S(2)}) async-start(), calls=%async_computation.3 | async-start | bytes 4456448 | tf_op jit(solution)/shard_map/all_gather | solution.py:80
  274.7 8.8 %copy-start.2 = (f32[1,1,64,2048]{3,2,1,0:T(8,128)S(1)}, f32[1,1,64,2048]{3,2,1,0:T(8,128)}, u32[]{:S(2)}) copy-start(f32[1,1,64,2048]{3,2,1,0:T(8,128)} %param.25) | copy-start | bytes 1572868
  286.0 0.8 copy-start.7
  300.8 6.1 %copy-start = (f32[6,64,2048]{2,1,0:T(8,128)S(1)}, f32[6,64,2048]{2,1,0:T(8,128)}, u32[]{:S(2)}) copy-start(f32[6,64,2048]{2,1,0:T(8,128)} %constant_dynamic-update-slice_fusion) | copy-start | bytes 9437188
  300.8 6.1 %copy-start.5 = (f32[64,2048]{1,0:T(8,128)S(1)}, f32[64,2048]{1,0:T(8,128)}, u32[]{:S(2)}) copy-start(f32[64,2048]{1,0:T(8,128)} %multiply_bitcast_fusion) | copy-start | bytes 1572868
  309.3 0.8 copy-start.8
  324.1 6.7 %copy-start.3 = (f32[1,1,64,2048]{3,2,1,0:T(8,128)S(1)}, f32[1,1,64,2048]{3,2,1,0:T(8,128)}, u32[]{:S(2)}) copy-start(f32[1,1,64,2048]{3,2,1,0:T(8,128)} %param.25) | copy-start | bytes 1572868
  333.3 0.8 copy-start.9
  348.5 5.9 %copy-start.1 = (f32[6,64,2048]{2,1,0:T(8,128)S(1)}, f32[6,64,2048]{2,1,0:T(8,128)}, u32[]{:S(2)}) copy-start(f32[6,64,2048]{2,1,0:T(8,128)} %constant_dynamic-update-slice_fusion) | copy-start | bytes 9437188
  348.5 5.9 %copy-start.6 = (f32[64,2048]{1,0:T(8,128)S(1)}, f32[64,2048]{1,0:T(8,128)}, u32[]{:S(2)}) copy-start(f32[64,2048]{1,0:T(8,128)} %multiply_bitcast_fusion) | copy-start | bytes 1572868
  356.8 0.8 copy-start.10
  374.1 8.4 %collective-permute-start.1 = (f32[1,64,2048]{2,1,0:T(8,128)}, f32[1,64,2048]{2,1,0:T(8,128)}, u32[]{:S(2)}, u32[]{:S(2)}) collective-permute-start(f32[1,64,2048]{2,1,0:T(8,128)} %bitcast.107), channel_id=1, source_target_pairs={{0,1},{1,0},{2,3},{3,2},{4,5},{5,4},{6,7},{7,6},{8,9},{9,8},{10,11... | collective-permute-start | bytes 1572872 | tf_op jit(solution)/shard_map/ppermute | solution.py:19
  374.1 5.2 %copy-start.4 = (f32[1,1,64,2048]{3,2,1,0:T(8,128)S(1)}, f32[1,1,64,2048]{3,2,1,0:T(8,128)}, u32[]{:S(2)}) copy-start(f32[1,1,64,2048]{3,2,1,0:T(8,128)} %param.25) | copy-start | bytes 1572868
  381.7 5.0 %collective-permute-start = (f32[1,64,2048]{2,1,0:T(8,128)S(1)}, f32[1,64,2048]{2,1,0:T(8,128)S(1)}, u32[]{:S(2)}, u32[]{:S(2)}) collective-permute-start(f32[1,64,2048]{2,1,0:T(8,128)S(1)} %convolution_bitcast_fusion), channel_id=1, source_target_pairs={{0,1},{1,0},{2,3},{3,2},{4,5},{5,4},{6,7},{7,6},{8,9},{9,8},{10,11... | collective-permute-start | bytes 1572872 | tf_op jit(solution)/shard_map/ppermute | solution.py:19
Sparse Core Ops, SparseCore 0:
  9.8 55.4 all-gather.4
  67.1 53.3 all-gather.8
  122.9 56.7 all-gather.6
  182.0 56.1 all-gather.10
where the time goes:
time: 466 us; the launch traced here: 461 us
  waiting for transfers between devices  186 us (40%)
  other arithmetic  115 us (25%)
  matrix products  81.8 us (18%)
  between operations  29 us (6%)
  blocking collectives  23.8 us (5%)
  local copies, waits for them, and re-layouts  23.2 us (5%)
    all_gather x1, waiting for transfers between devices, shards(): lax.all_gather(right_v, 'rows', axis=1, tiled=True)  59.2 us
    dot_general x28, matrix products, cross(): lax.dot_general(first, second, (((dim_first,), (dim_second,)), ((), ())),...  57.2 us
    all_gather x1, waiting for transfers between devices, shards(): lax.all_gather(left_u, 'cols', axis=1, tiled=True)  55.2 us
    all_gather x1, waiting for transfers between devices, shards(): lax.all_gather(right_u, 'rows', axis=1, tiled=True)  54.2 us
    another operation x24, other arithmetic, orthonormal(): lower = lax.linalg.cholesky(gram)  52.5 us
    another operation x16, other arithmetic, orthonormal(): lax.linalg.triangular_solve(lower, rows_t, left_side=True, lower=True)  44.4 us
    unnamed x2, blocking collectives  23.8 us
    unnamed x33, local copies, waits for them, and re-layouts  15.5 us
  transfers between devices with their start and end apart: 6, of which 4 were waited for; matrix products, arithmetic and copies ran while one was open for 5% of the time, Pallas kernels for 0%

commit v1 on v0

--- a/solution.py
+++ b/solution.py
@@ -72,7 +72,9 @@
     tcols = tile_left.shape[1]
     slots = triples.shape[3]
     row_u, row_v, row_rank = (
-        lax.all_gather(left_u, "cols", axis=1, tiled=True),
+        jnp.concatenate(
+            lax.all_to_all(jnp.stack([left_u] * lax.axis_size("cols")), "cols", 0, 0), axis=1
+        ),
         lax.all_gather(left_v, "cols", axis=1, tiled=True),
         lax.all_gather(rank_left, "cols", axis=1, tiled=True),
     )

time: 466 us -> 498 us (1.069)
  blocking collectives: 23.8 us -> 126 us
  waiting for transfers between devices: 186 us -> 109 us
  starting transfers between devices: 0.92 us -> 9.03 us
    unnamed x2, blocking collectives: 23.8 us -> 126 us
    all_gather x1 -> x0, waiting for transfers between devices: 55.2 us -> none  [shards(): lax.all_gather(left_u, 'cols', axis=1, tiled=True)]
    all_gather x1, waiting for transfers between devices: 15.1 us -> 0.01 us  [shards(): lax.all_gather(left_v, 'cols', axis=1, tiled=True)]
    all_to_all x0 -> x1, starting transfers between devices: none -> 8.15 us  [shards(): lax.all_to_all(jnp.stack([left_u] * lax.axis_size('cols')), 'cols', 0, 0)]
    all_gather x1, waiting for transfers between devices: 59.2 us -> 52.7 us  [shards(): lax.all_gather(right_v, 'rows', axis=1, tiled=True)]
    unnamed x33 -> x43, local copies, waits for them, and re-layouts: 15.5 us -> 13.5 us
  transfers between devices with their start and end apart: 6 -> 6, of which waited for: 4 -> 2; matrix products, arithmetic and copies ran while one was open for 5% -> 5% of each run, Pallas kernels for 0% -> 0%
where the time goes in v1:
time: 498 us; the launch traced here: 493 us
  blocking collectives  126 us (25%)
  other arithmetic  114 us (23%)
  waiting for transfers between devices  109 us (22%)
  matrix products  81.5 us (16%)
  between operations  29.1 us (6%)
  local copies, waits for them, and re-layouts  23.8 us (5%)
  starting transfers between devices  9.03 us (2%)
    unnamed x2, blocking collectives  126 us
    dot_general x28, matrix products, cross(): lax.dot_general(first, second, (((dim_first,), (dim_second,)), ((), ())),...  57.1 us
    all_gather x1, waiting for transfers between devices, shards(): lax.all_gather(right_u, 'rows', axis=1, tiled=True)  54.3 us
    all_gather x1, waiting for transfers between devices, shards(): lax.all_gather(right_v, 'rows', axis=1, tiled=True)  52.7 us
    another operation x24, other arithmetic, orthonormal(): lower = lax.linalg.cholesky(gram)  52.5 us
    another operation x16, other arithmetic, orthonormal(): lax.linalg.triangular_solve(lower, rows_t, left_side=True, lower=True)  44.4 us
    dot_general x6, matrix products, slot_term(): lax.dot_general(inner, outer_left, (((0,), (0,)), ((), ())), preferred_el...  14 us
    unnamed x43, local copies, waits for them, and re-layouts  13.5 us
  transfers between devices with their start and end apart: 6, of which 2 were waited for; matrix products, arithmetic and copies ran while one was open for 5% of the time, Pallas kernels for 0%

profile of v1, /device:TPU:57, one launch (start us, length us, event | category | flops | bytes accessed | tf_op | source)
XLA Modules:
  0.0 492.9 jit_solution(12095099587616378156)
XLA Ops:
  9.4 3.5 stack.73
  12.9 8.2 %all-to-all-start = ((bf16[8,1,2,1,64,2048]{5,4,2,3,1,0:T(8,128)(2,1)}), bf16[8,1,2,1,64,2048]{5,4,2,3,1,0:T(8,128)(2,1)}, u32[]{:S(2)}, u32[]{:S(2)}) async-start(bf16[8,1,2,1,64,2048]{5,4,2,3,1,0:T(8,128)(2,1)} %stack.73), calls=%async_computation | async-start | bytes 8388608 | tf_op jit(solution)/shard_map/all_to_all | solution.py:76
  23.0 11.6 %all-reduce.1 = s32[16]{0:T(128)S(1)} all-reduce(s32[16]{0:T(128)S(1)} %bitcast_dynamic-update-slice_fusion.6), channel_id=1, replica_groups=mesh['rows'=16,'cols'=8,'depth'=2] {'rows'}, use_global_device_ids=true, to_apply=%add.1 | all-reduce | flops 16 | bytes 128
  44.5 113.9 %all-reduce = s32[16]{0:T(128)S(1)} all-reduce(s32[16]{0:T(128)S(1)} %bitcast_dynamic-update-slice_fusion.7), channel_id=1, replica_groups=mesh['rows'=16,'cols'=8,'depth'=2] {'cols'}, use_global_device_ids=true, to_apply=%add | all-reduce | flops 16 | bytes 128
  159.2 52.7 %all-gather.6.cloned.1.call-done = bf16[1,16,1,64,2048]{4,3,2,0,1:T(8,128)(2,1)} async-done(((bf16[1,1,1,64,2048]{4,3,2,0,1:T(8,128)(2,1)}), bf16[1,16,1,64,2048]{4,3,2,0,1:T(8,128)(2,1)}) %all-gather.6.cloned.1.call-update) | async-done | bytes 4194320 | tf_op jit(solution)/shard_map/all_gather | solution.py:83
  212.0 3.5 conditional.6
  216.3 54.3 %all-gather.8.cloned.1.call-done = bf16[1,16,1,64,2048]{4,3,2,0,1:T(8,128)(2,1)} async-done(((bf16[1,1,1,64,2048]{4,3,2,0,1:T(8,128)(2,1)}), bf16[1,16,1,64,2048]{4,3,2,0,1:T(8,128)(2,1)}) %all-gather.8.cloned.1.call-update) | async-done | bytes 4194320 | tf_op jit(solution)/shard_map/all_gather | solution.py:82
  277.1 4.4 conditional.7
  279.0 2.5 fusion.19
  283.4 4.4 conditional.8
  285.3 2.5 fusion.38
  287.8 1.9 constant_dynamic-update-slice_fusion.3
  289.7 4.4 conditional.9
  291.6 2.5 fusion.57
  294.0 1.9 constant_dynamic-update-slice_fusion.2
  295.9 4.4 conditional.10
  297.8 2.5 fusion.76
  302.2 4.8 conditional.11
  304.1 2.5 fusion.95
  307.0 2.0 constant_dynamic-update-slice_fusion
  309.0 6.8 %fusion.122 = f32[448,64]{1,0:T(8,128)S(1)} fusion(f32[384,2048]{1,0:T(8,128)} %bitcast.305, f32[64,2048]{1,0:T(8,128)} %multiply_bitcast_fusion, s32[2048]{0:T(1024)S(1)} %multiply_add_fusion, s32[64]{0:T(128)S(1)} %iota_add_fusion), kind=kOutput, calls=%fused_computation.132 | convolution fusion | flops 707395584 | bytes 3793152 | tf_op jit(solution)/shard_map/dot_general | solution.py:23
  315.8 2.4 fusion.117
  321.0 5.8 %custom-call.20 = f32[64,64]{1,0:T(8,128)S(1)} custom-call(f32[64,64]{1,0:T(8,128)S(1)} %fusion.180), custom_call_target="Cholesky" | custom-call | tf_op jit(solution)/shard_map/cholesky/custom-call.1 | solution.py:43
  328.1 4.9 custom-call.21
  334.9 4.2 fusion.116
  339.2 2.4 fusion.121
  344.3 5.8 %custom-call.22 = f32[64,64]{1,0:T(8,128)S(1)} custom-call(f32[64,64]{1,0:T(8,128)S(1)} %fusion.176), custom_call_target="Cholesky" | custom-call | tf_op jit(solution)/shard_map/cholesky/custom-call.1 | solution.py:43
  351.5 4.9 custom-call.23
  358.1 5.0 %fusion.120 = f32[448,64]{1,0:T(8,128)S(1)} fusion(f32[64,2048]{1,0:T(8,128)S(1)} %fusion.173, f32[384,2048]{1,0:T(8,128)} %bitcast.306, f32[64,2048]{1,0:T(8,128)} %multiply_bitcast_fusion), kind=kOutput, calls=%fused_computation.130 | convolution fusion | flops 705560576 | bytes 4308992 | tf_op jit(solution)/shard_map/dot_general | solution.py:23
  363.1 2.4 fusion.115
  368.2 6.2 %custom-call.24 = f32[64,64]{1,0:T(8,128)S(1)} custom-call(f32[64,64]{1,0:T(8,128)S(1)} %fusion.172), custom_call_target="Cholesky" | custom-call | tf_op jit(solution)/shard_map/cholesky/custom-call.1 | solution.py:43
  375.8 4.9 custom-call.25
  382.5 4.0 fusion.114
  386.6 2.4 fusion.119
  391.8 5.8 %custom-call.26 = f32[64,64]{1,0:T(8,128)S(1)} custom-call(f32[64,64]{1,0:T(8,128)S(1)} %fusion.168), custom_call_target="Cholesky" | custom-call | tf_op jit(solution)/shard_map/cholesky/custom-call.1 | solution.py:43
  398.9 4.9 custom-call.27
  403.8 2.5 fusion.165
  406.3 5.2 %fusion.118 = f32[448,64]{1,0:T(8,128)S(1)} fusion(f32[64,2048]{1,0:T(8,128)} %fusion.165, f32[384,2048]{1,0:T(8,128)} %bitcast.307, f32[64,2048]{1,0:T(8,128)} %multiply_bitcast_fusion), kind=kOutput, calls=%fused_computation.128 | convolution fusion | flops 705560576 | bytes 4308992 | tf_op jit(solution)/shard_map/dot_general | solution.py:23
  411.5 2.4 convolution_bitcast_fusion
  416.0 3.0 fusion.131
  421.7 5.8 %custom-call.28 = f32[64,64]{1,0:T(8,128)S(1)} custom-call(f32[64,64]{1,0:T(8,128)S(1)} %fusion.164), custom_call_target="Cholesky" | custom-call | tf_op jit(solution)/shard_map/cholesky/custom-call.1 | solution.py:43
  428.9 4.9 custom-call.29
  438.1 5.8 %custom-call.30 = f32[64,64]{1,0:T(8,128)S(1)} custom-call(f32[64,64]{1,0:T(8,128)S(1)} %fusion.160), custom_call_target="Cholesky" | custom-call | tf_op jit(solution)/shard_map/cholesky/custom-call.1 | solution.py:43
  445.2 4.9 custom-call.31
  454.6 5.8 %custom-call.32 = f32[64,64]{1,0:T(8,128)S(1)} custom-call(f32[64,64]{1,0:T(8,128)S(1)} %fusion.156), custom_call_target="Cholesky" | custom-call | tf_op jit(solution)/shard_map/cholesky/custom-call.1 | solution.py:43
  461.8 4.9 custom-call.33
  470.9 5.8 %custom-call.34 = f32[64,64]{1,0:T(8,128)S(1)} custom-call(f32[64,64]{1,0:T(8,128)S(1)} %fusion.152), custom_call_target="Cholesky" | custom-call | tf_op jit(solution)/shard_map/cholesky/custom-call.1 | solution.py:43
  478.1 4.9 custom-call.35
  (150 shorter events, 71.9 us)
Async XLA Ops:
  7.2 152.1 %all-gather.4.cloned.1.call-start = ((), (), s32[]{:S(2)}) async-start(), calls=%async_computation.1 | async-start | bytes 4718592 | tf_op jit(solution)/shard_map/all_gather | solution.py:78
  7.9 204.1 %all-gather.6.cloned.1.call-start = ((), (), s32[]{:S(2)}) async-start(), calls=%async_computation.2 | async-start | bytes 4456448 | tf_op jit(solution)/shard_map/all_gather | solution.py:83
  8.6 262.0 %all-gather.8.cloned.1.call-start = ((), (), s32[]{:S(2)}) async-start(), calls=%async_computation.3 | async-start | bytes 4456448 | tf_op jit(solution)/shard_map/all_gather | solution.py:82
  12.9 8.8 %copy-start.15 = (u32[256]{0:T(256)S(1)}, u32[256]{0:T(256)}, u32[]{:S(2)}) copy-start(u32[256]{0:T(256)} %constant.201) | copy-start | bytes 3076
  12.9 21.7 %copy-start.12 = (s32[1,1,1,6]{3,2,1,0:T(1,128)S(1)}, s32[1,1,1,6]{3,2,1,0:T(1,128)}, u32[]{:S(2)}) copy-start(s32[1,1,1,6]{3,2,1,0:T(1,128)} %param.32) | copy-start | bytes 76
  12.9 30.2 %copy-start.14 = (u32[256]{0:T(256)S(1)}, u32[256]{0:T(256)}, u32[]{:S(2)}) copy-start(u32[256]{0:T(256)} %constant.196) | copy-start | bytes 3076
  12.9 31.5 %copy-start.13 = (s32[1,2,1]{1,2,0:T(1,128)S(1)}, s32[1,2,1]{1,2,0:T(1,128)}, u32[]{:S(2)}) copy-start(s32[1,2,1]{1,2,0:T(1,128)} %param.28) | copy-start | bytes 28
  12.9 145.5 %copy-start.11 = (f32[1,1,64,2048]{3,2,1,0:T(8,128)S(1)}, f32[1,1,64,2048]{3,2,1,0:T(8,128)}, u32[]{:S(2)}) copy-start(f32[1,1,64,2048]{3,2,1,0:T(8,128)} %param.24) | copy-start | bytes 1572868
  12.9 146.3 %all-to-all-start = ((bf16[8,1,2,1,64,2048]{5,4,2,3,1,0:T(8,128)(2,1)}), bf16[8,1,2,1,64,2048]{5,4,2,3,1,0:T(8,128)(2,1)}, u32[]{:S(2)}, u32[]{:S(2)}) async-start(bf16[8,1,2,1,64,2048]{5,4,2,3,1,0:T(8,128)(2,1)} %stack.73), calls=%async_computation | async-start | bytes 8388608 | tf_op jit(solution)/shard_map/all_to_all | solution.py:76
  307.0 8.8 %copy-start.2 = (f32[1,1,64,2048]{3,2,1,0:T(8,128)S(1)}, f32[1,1,64,2048]{3,2,1,0:T(8,128)}, u32[]{:S(2)}) copy-start(f32[1,1,64,2048]{3,2,1,0:T(8,128)} %param.25) | copy-start | bytes 1572868
  318.3 0.8 copy-start.7
  333.0 6.1 %copy-start = (f32[6,64,2048]{2,1,0:T(8,128)S(1)}, f32[6,64,2048]{2,1,0:T(8,128)}, u32[]{:S(2)}) copy-start(f32[6,64,2048]{2,1,0:T(8,128)} %constant_dynamic-update-slice_fusion) | copy-start | bytes 9437188
  333.1 6.1 %copy-start.5 = (f32[64,2048]{1,0:T(8,128)S(1)}, f32[64,2048]{1,0:T(8,128)}, u32[]{:S(2)}) copy-start(f32[64,2048]{1,0:T(8,128)} %multiply_bitcast_fusion) | copy-start | bytes 1572868
  341.6 0.8 copy-start.8
  356.4 6.7 %copy-start.3 = (f32[1,1,64,2048]{3,2,1,0:T(8,128)S(1)}, f32[1,1,64,2048]{3,2,1,0:T(8,128)}, u32[]{:S(2)}) copy-start(f32[1,1,64,2048]{3,2,1,0:T(8,128)} %param.25) | copy-start | bytes 1572868
  365.5 0.8 copy-start.9
  380.7 5.9 %copy-start.1 = (f32[6,64,2048]{2,1,0:T(8,128)S(1)}, f32[6,64,2048]{2,1,0:T(8,128)}, u32[]{:S(2)}) copy-start(f32[6,64,2048]{2,1,0:T(8,128)} %constant_dynamic-update-slice_fusion) | copy-start | bytes 9437188
  380.7 5.9 %copy-start.6 = (f32[64,2048]{1,0:T(8,128)S(1)}, f32[64,2048]{1,0:T(8,128)}, u32[]{:S(2)}) copy-start(f32[64,2048]{1,0:T(8,128)} %multiply_bitcast_fusion) | copy-start | bytes 1572868
  389.0 0.8 copy-start.10
  406.3 8.4 %collective-permute-start.1 = (f32[1,64,2048]{2,1,0:T(8,128)}, f32[1,64,2048]{2,1,0:T(8,128)}, u32[]{:S(2)}, u32[]{:S(2)}) collective-permute-start(f32[1,64,2048]{2,1,0:T(8,128)} %bitcast.108), channel_id=1, source_target_pairs={{0,1},{1,0},{2,3},{3,2},{4,5},{5,4},{6,7},{7,6},{8,9},{9,8},{10,11... | collective-permute-start | bytes 1572872 | tf_op jit(solution)/shard_map/ppermute | solution.py:19
  406.3 5.2 %copy-start.4 = (f32[1,1,64,2048]{3,2,1,0:T(8,128)S(1)}, f32[1,1,64,2048]{3,2,1,0:T(8,128)}, u32[]{:S(2)}) copy-start(f32[1,1,64,2048]{3,2,1,0:T(8,128)} %param.25) | copy-start | bytes 1572868
  414.0 5.1 %collective-permute-start = (f32[1,64,2048]{2,1,0:T(8,128)S(1)}, f32[1,64,2048]{2,1,0:T(8,128)S(1)}, u32[]{:S(2)}, u32[]{:S(2)}) collective-permute-start(f32[1,64,2048]{2,1,0:T(8,128)S(1)} %convolution_bitcast_fusion), channel_id=1, source_target_pairs={{0,1},{1,0},{2,3},{3,2},{4,5},{5,4},{6,7},{7,6},{8,9},{9,8},{10,11... | collective-permute-start | bytes 1572872 | tf_op jit(solution)/shard_map/ppermute | solution.py:19
Sparse Core Ops, SparseCore 0:
  9.8 140.4 all-gather.3
  152.7 59.2 all-gather.5
  214.4 56.1 all-gather.7
